TPU v7x, 32 devices: a whole 2x2x4 slice. The times are simulated.
32 devices in a mesh: dp: 8 (over z, x), tensor: 4 (over y, core).
Axes of the slice: x: 2, y: 2, z: 4, core: 2. Of those that a mesh axis runs over, the one named last changes fastest.
Arguments:
- inputs: bfloat16 [16384, 768], P(('dp', 'tensor')), may hold values from -6 to 6
- teacher: bfloat16 [16384, 768], P(('dp', 'tensor')), may hold values from -6 to 6
- lengths: int32 [8], P('dp'), may hold values from 512 to 2048
- buckets: int32 [4096], replicated, may hold values from 0 to 31
- gain_attn: bfloat16 [768], replicated, may hold values from 0.25 to 1.75
- w_query: bfloat16 [768, 768], P(None, 'tensor'), may hold values from -0.4375 to 0.4375
- w_key: bfloat16 [768, 768], P(None, 'tensor'), may hold values from -0.21875 to 0.21875
- w_value: bfloat16 [768, 768], P(None, 'tensor'), may hold values from -0.21875 to 0.21875
- w_out: bfloat16 [768, 768], P('tensor'), may hold values from -1.75 to 1.75
- bias_table: bfloat16 [32, 12], P(None, 'tensor'), may hold values from -4 to 4
- gain_ff: bfloat16 [768], replicated, may hold values from 0.25 to 1.75
- w_gate: bfloat16 [768, 2048], P(None, 'tensor'), may hold values from -0.21875 to 0.21875
- w_up: bfloat16 [768, 2048], P(None, 'tensor'), may hold values from -0.21875 to 0.21875
- w_down: bfloat16 [2048, 768], P('tensor'), may hold values from -0.125 to 0.125
Outputs:
- activations: bfloat16 [16384, 768], P(('dp', 'tensor'))
- loss: float32 [], replicated
- grad_inputs: float32 [16384, 768], P(('dp', 'tensor'))
- grad_gain_attn: float32 [768], replicated
- grad_query: float32 [768, 768], P(None, 'tensor')
- grad_key: float32 [768, 768], P(None, 'tensor')
- grad_value: float32 [768, 768], P(None, 'tensor')
- grad_out: float32 [768, 768], P('tensor')
- grad_table: float32 [32, 12], P(None, 'tensor')
- grad_gain_ff: float32 [768], replicated
- grad_gate: float32 [768, 2048], P(None, 'tensor')
- grad_up: float32 [768, 2048], P(None, 'tensor')
- grad_down: float32 [2048, 768], P('tensor')
All inputs are finite; a program needn't handle non-finite values.
Results may differ from a plain program's by a relative error of at most 0.015.
The roundings to bfloat16 on the way count: a program that leaves them out, or rounds other values in their place, can miss the bound.
Values may be sent and summed in bfloat16 or wider, within the bound.
A program may use at most 320 MiB of HBM per device.

v0:
```python
import jax
import jax.numpy as jnp
from jax import lax
from jax.sharding import PartitionSpec as P

QBLOCK = 512
eps_norm = 1e-06
masked_score = -1e30
highest = lax.Precision.HIGHEST
contract_rows = (((0,), (0,)), ((), ()))
contract_cols = (((1,), (1,)), ((), ()))
contract_table = (((0,), (1,)), ((), ()))


def row_norm(values, gain):
    inverse = lax.rsqrt(jnp.mean(values * values, axis=-1, keepdims=True) + eps_norm)
    return values * inverse * gain


def geglu_mask(gate_values, up_values, keep_column):
    return keep_column * jax.nn.gelu(gate_values, approximate=True) * up_values


def valid_mask(lengths, first_row, row_count, seq_len):
    positions = first_row + lax.iota(jnp.int32, row_count)
    owners = positions // seq_len
    within = positions % seq_len
    chosen = owners[:, None] == lax.iota(jnp.int32, lengths.shape[0])[None, :]
    limits = jnp.sum(jnp.where(chosen, lengths[None, :], 0), axis=1)
    return (within < limits).astype(jnp.float32)


def bucket_rows(buckets, bias_table):
    one_hot = (buckets[:, None] == lax.iota(jnp.int32, bias_table.shape[0])[None, :]).astype(
        jnp.float32
    )
    relative = lax.dot_general(
        bias_table.astype(jnp.float32), one_hot, contract_table, precision=highest
    )
    return (one_hot, relative)


def band_matrix(window, block_rows, seq_len):
    heads_here = window.shape[0]
    span = seq_len + block_rows - 1
    tiled = jnp.tile(window, (1, block_rows + 1))
    tiled = tiled[:, block_rows - 1 : block_rows - 1 + block_rows * (span - 1)]
    return tiled.reshape(heads_here, block_rows, span - 1)[:, :, :seq_len]


def make_bands(relative, block_rows, seq_len):
    pieces = []
    for block_index in range(seq_len // block_rows):
        first_row = block_index * block_rows
        start = seq_len - first_row - block_rows + 1
        window = relative[:, start : start + seq_len + block_rows - 1]
        pieces.append(band_matrix(window, block_rows, seq_len))
    return jnp.stack(pieces, axis=1)


def attend_head(query_head, key_head, value_head, keep_seq, length, bands_head, block_rows, scale):
    seq_len, head_dim = query_head.shape
    key_live = lax.iota(jnp.int32, seq_len) < length

    def one_block(step_index, totals):
        mixed_rows, log_sums = totals
        first_row = step_index * block_rows
        query_block = lax.dynamic_slice_in_dim(query_head, first_row, block_rows, 0)
        band = lax.dynamic_index_in_dim(bands_head, step_index, 0, keepdims=False)
        raw_scores = lax.dot_general(
            query_block, key_head, contract_cols, preferred_element_type=jnp.float32
        )
        scores = jnp.where(key_live[None, :], raw_scores * scale + band, masked_score)
        row_max = jnp.max(scores, axis=-1, keepdims=True)
        expos = jnp.exp(scores - row_max)
        row_total = jnp.sum(expos, axis=-1, keepdims=True)
        probs = (expos / row_total).astype(jnp.bfloat16)
        mixed = jnp.dot(probs, value_head, preferred_element_type=jnp.float32)
        keep_block = lax.dynamic_slice_in_dim(keep_seq, first_row, block_rows, 0)
        mixed = (mixed * keep_block[:, None]).astype(jnp.bfloat16)
        mixed_rows = lax.dynamic_update_slice_in_dim(mixed_rows, mixed, first_row, 0)
        log_sums = lax.dynamic_update_slice_in_dim(
            log_sums, (row_max + jnp.log(row_total))[:, 0], first_row, 0
        )
        return (mixed_rows, log_sums)

    initial = (jnp.zeros((seq_len, head_dim), jnp.bfloat16), jnp.zeros((seq_len,), jnp.float32))
    return lax.fori_loop(0, seq_len // block_rows, one_block, initial)


def attend_head_back(
    query_head,
    key_head,
    value_head,
    grad_head,
    log_sums,
    length,
    bands_head,
    grad_bands_head,
    block_rows,
    scale,
):
    seq_len, head_dim = query_head.shape
    key_live = lax.iota(jnp.int32, seq_len) < length

    def one_block(step_index, totals):
        grad_query, grad_key, grad_value, grad_band = totals
        first_row = step_index * block_rows
        query_block = lax.dynamic_slice_in_dim(query_head, first_row, block_rows, 0)
        grad_block = lax.dynamic_slice_in_dim(grad_head, first_row, block_rows, 0)
        band = lax.dynamic_index_in_dim(bands_head, step_index, 0, keepdims=False)
        raw_scores = lax.dot_general(
            query_block, key_head, contract_cols, preferred_element_type=jnp.float32
        )
        scores = jnp.where(key_live[None, :], raw_scores * scale + band, masked_score)
        block_sums = lax.dynamic_slice_in_dim(log_sums, first_row, block_rows, 0)
        probs = jnp.exp(scores - block_sums[:, None])
        grad_value = grad_value + lax.dot_general(
            probs.astype(jnp.bfloat16),
            grad_block,
            contract_rows,
            preferred_element_type=jnp.float32,
        )
        grad_probs = lax.dot_general(
            grad_block, value_head, contract_cols, preferred_element_type=jnp.float32
        )
        inner = jnp.sum(probs * grad_probs, axis=-1, keepdims=True)
        grad_scores = (probs * (grad_probs - inner)).astype(jnp.bfloat16)
        grad_query_block = (
            jnp.dot(grad_scores, key_head, preferred_element_type=jnp.float32) * scale
        )
        grad_query = lax.dynamic_update_slice_in_dim(
            grad_query, grad_query_block.astype(jnp.bfloat16), first_row, 0
        )
        grad_key = (
            grad_key
            + lax.dot_general(
                grad_scores, query_block, contract_rows, preferred_element_type=jnp.float32
            )
            * scale
        )
        current = lax.dynamic_index_in_dim(grad_band, step_index, 0, keepdims=True)
        grad_band = lax.dynamic_update_slice_in_dim(
            grad_band, current + grad_scores.astype(jnp.float32)[None], step_index, 0
        )
        return (grad_query, grad_key, grad_value, grad_band)

    initial = (
        jnp.zeros((seq_len, head_dim), jnp.bfloat16),
        jnp.zeros((seq_len, head_dim), jnp.float32),
        jnp.zeros((seq_len, head_dim), jnp.float32),
        grad_bands_head,
    )
    return lax.fori_loop(0, seq_len // block_rows, one_block, initial)


def on_device(
    inputs,
    teacher,
    lengths,
    buckets,
    gain_attn,
    w_query,
    w_key,
    w_value,
    w_out,
    bias_table,
    gain_ff,
    w_gate,
    w_up,
    w_down,
):
    row_count, model_width = inputs.shape
    group_size = lax.axis_size("tensor")
    seq_len = buckets.shape[0] // 2
    all_rows = row_count * group_size
    block_rows = QBLOCK
    local_width = w_query.shape[1]
    heads_here = bias_table.shape[1]
    head_dim = local_width // heads_here
    ff_width = w_gate.shape[1]
    scale = head_dim ** (-0.5)
    my_first = lax.axis_index("tensor") * row_count
    keep_mine = valid_mask(lengths, my_first, row_count, seq_len)
    keep_all = valid_mask(lengths, 0, all_rows, seq_len)
    one_hot, relative = bucket_rows(buckets, bias_table)
    bands = make_bands(relative, block_rows, seq_len)
    gain_a = gain_attn.astype(jnp.float32)
    gain_f = gain_ff.astype(jnp.float32)
    source = inputs.astype(jnp.float32)
    normed = row_norm(source, gain_a).astype(jnp.bfloat16)
    normed_all = lax.all_gather(normed, "tensor", axis=0, tiled=True)
    w_joint = jnp.concatenate([w_query, w_key, w_value], axis=1)

    def head_proj(weight, head):
        columns = weight[:, head * head_dim : (head + 1) * head_dim]
        return jnp.dot(normed_all, columns, preferred_element_type=jnp.float32).astype(jnp.bfloat16)

    query_heads = [head_proj(w_query, head) for head in range(heads_here)]
    key_heads = [head_proj(w_key, head) for head in range(heads_here)]
    value_heads = [head_proj(w_value, head) for head in range(heads_here)]
    seq_index = 0
    head_mixed = []
    head_sums = []
    for head in range(heads_here):
        mixed_head, sums_head = attend_head(
            query_heads[head],
            key_heads[head],
            value_heads[head],
            keep_all,
            lengths[seq_index],
            bands[head],
            block_rows,
            scale,
        )
        head_mixed.append(mixed_head)
        head_sums.append(sums_head)
    mixed_parts = jnp.concatenate(head_mixed, axis=1)
    sums_parts = [head_sums]
    middle = source + lax.psum_scatter(
        jnp.dot(mixed_parts, w_out, preferred_element_type=jnp.float32).astype(jnp.bfloat16),
        "tensor",
        scatter_dimension=0,
        tiled=True,
    ).astype(jnp.float32)
    normed_ff = row_norm(middle, gain_f).astype(jnp.bfloat16)
    normed_ff_all = lax.all_gather(normed_ff, "tensor", axis=0, tiled=True)
    w_pair = jnp.concatenate([w_gate, w_up], axis=1)
    paired = jnp.dot(normed_ff_all, w_pair, preferred_element_type=jnp.float32)
    gate_values = paired[:, :ff_width]
    up_values = paired[:, ff_width:]
    hidden = geglu_mask(gate_values, up_values, keep_all[:, None]).astype(jnp.bfloat16)
    output = middle + lax.psum_scatter(
        jnp.dot(hidden, w_down, preferred_element_type=jnp.float32).astype(jnp.bfloat16),
        "tensor",
        scatter_dimension=0,
        tiled=True,
    ).astype(jnp.float32)
    activations = output.astype(jnp.bfloat16)
    cotangent = keep_mine[:, None] * (output - teacher.astype(jnp.float32))
    loss_part = jnp.sum(cotangent * cotangent)
    count_part = jnp.sum(keep_mine)
    shard_piece = lax.all_gather(cotangent.astype(jnp.bfloat16), "tensor", axis=0, tiled=True)
    grad_down_acc = lax.dot_general(
        hidden, shard_piece, contract_rows, preferred_element_type=jnp.float32
    )
    grad_rows = lax.dot_general(
        shard_piece, w_down, contract_cols, preferred_element_type=jnp.float32
    )
    grad_down = grad_down_acc
    grad_hidden = grad_rows
    _, geglu_back = jax.vjp(
        lambda gate_in, up_in: geglu_mask(gate_in, up_in, keep_all[:, None]), gate_values, up_values
    )
    grad_gate_rows, grad_up_rows = geglu_back(grad_hidden)
    grad_pair = jnp.concatenate([grad_gate_rows, grad_up_rows], axis=1).astype(jnp.bfloat16)
    grad_w_pair = lax.dot_general(
        normed_ff_all, grad_pair, contract_rows, preferred_element_type=jnp.float32
    )
    grad_normed_ff = lax.psum_scatter(
        lax.dot_general(
            grad_pair, w_pair, contract_cols, preferred_element_type=jnp.float32
        ).astype(jnp.bfloat16),
        "tensor",
        scatter_dimension=0,
        tiled=True,
    ).astype(jnp.float32)
    _, norm_back_ff = jax.vjp(row_norm, middle, gain_f)
    grad_middle_part, grad_gain_ff = norm_back_ff(grad_normed_ff)
    grad_middle = cotangent + grad_middle_part
    shard_piece = lax.all_gather(grad_middle.astype(jnp.bfloat16), "tensor", axis=0, tiled=True)
    grad_out_acc = lax.dot_general(
        mixed_parts, shard_piece, contract_rows, preferred_element_type=jnp.float32
    )
    grad_rows = lax.dot_general(
        shard_piece, w_out, contract_cols, preferred_element_type=jnp.float32
    )
    grad_out = grad_out_acc
    grad_mix = grad_rows.astype(jnp.bfloat16) * keep_all[:, None].astype(jnp.bfloat16)
    grad_bands = [jnp.zeros(bands.shape[1:], jnp.float32) for head in range(heads_here)]
    seq_index = 0
    low_row = seq_index * seq_len
    query_grads = []
    key_grads = []
    value_grads = []
    for head in range(heads_here):
        grad_head = grad_mix[low_row : low_row + seq_len, head * head_dim : (head + 1) * head_dim]
        grad_q, grad_k, grad_v, grad_bands[head] = attend_head_back(
            query_heads[head],
            key_heads[head],
            value_heads[head],
            grad_head,
            sums_parts[seq_index][head],
            lengths[seq_index],
            bands[head],
            grad_bands[head],
            block_rows,
            scale,
        )
        query_grads.append(grad_q)
        key_grads.append(grad_k.astype(jnp.bfloat16))
        value_grads.append(grad_v.astype(jnp.bfloat16))
    grad_parts = jnp.concatenate(query_grads + key_grads + value_grads, axis=1)
    _, bands_back = jax.vjp(lambda values: make_bands(values, block_rows, seq_len), relative)
    (grad_relative,) = bands_back(jnp.stack(grad_bands, axis=0))
    grad_w_joint = lax.dot_general(
        normed_all, grad_parts, contract_rows, preferred_element_type=jnp.float32
    )
    grad_table = lax.dot_general(one_hot, grad_relative, contract_table, precision=highest)
    grad_normed = lax.psum_scatter(
        lax.dot_general(
            grad_parts, w_joint, contract_cols, preferred_element_type=jnp.float32
        ).astype(jnp.bfloat16),
        "tensor",
        scatter_dimension=0,
        tiled=True,
    ).astype(jnp.float32)
    _, norm_back_attn = jax.vjp(row_norm, source, gain_a)
    grad_source_part, grad_gain_attn = norm_back_attn(grad_normed)
    grad_source = grad_middle + grad_source_part
    gain_attn_total, gain_ff_total, loss_total, count_total = lax.psum(
        (grad_gain_attn, grad_gain_ff, loss_part, count_part), ("dp", "tensor")
    )
    grad_w_joint, grad_out, grad_table, grad_w_pair, grad_down = lax.psum(
        (grad_w_joint, grad_out, grad_table, grad_w_pair, grad_down), "dp"
    )
    factor = 2.0 / (count_total * model_width)
    loss = loss_total / (count_total * model_width)
    return (
        activations,
        loss,
        grad_source * factor,
        gain_attn_total * factor,
        grad_w_joint[:, :local_width] * factor,
        grad_w_joint[:, local_width : 2 * local_width] * factor,
        grad_w_joint[:, 2 * local_width :] * factor,
        grad_out * factor,
        grad_table * factor,
        gain_ff_total * factor,
        grad_w_pair[:, :ff_width] * factor,
        grad_w_pair[:, ff_width:] * factor,
        grad_down * factor,
    )


def solution(mesh):
    in_specs = (
        P(("dp", "tensor"), None),
        P(("dp", "tensor"), None),
        P("dp"),
        P(),
        P(),
        P(None, "tensor"),
        P(None, "tensor"),
        P(None, "tensor"),
        P("tensor", None),
        P(None, "tensor"),
        P(),
        P(None, "tensor"),
        P(None, "tensor"),
        P("tensor", None),
    )
    out_specs = (
        P(("dp", "tensor"), None),
        P(),
        P(("dp", "tensor"), None),
        P(),
        P(None, "tensor"),
        P(None, "tensor"),
        P(None, "tensor"),
        P("tensor", None),
        P(None, "tensor"),
        P(),
        P(None, "tensor"),
        P(None, "tensor"),
        P("tensor", None),
    )
    return jax.shard_map(
        on_device, mesh=mesh, in_specs=in_specs, out_specs=out_specs, check_vma=False
    )
```

profile of v0, /device:TPU:12, one launch (start us, length us, event | category | flops | bytes accessed | tf_op | source)
XLA Modules:
  0.0 2143.7 jit_solution(9181588129690975066)
XLA Ops:
  22.7 24.2 %reshape.252 = f32[3938301]{0:T(1024)} reshape(f32[3,513,2559]{2,1,0:T(8,128)} %tile.40) | data formatting | bytes 31506408
  46.9 23.7 %tile.41 = f32[3,1312767]{1,0:T(4,128)} reshape(f32[3938301]{0:T(1024)} %reshape.252) | data formatting | bytes 31506408 | tf_op jit(solution)/shard_map/tile | solution.py:46
  70.6 21.8 %slice.146 = f32[3,1309696]{1,0:T(4,128)} slice(f32[3,1312767]{1,0:T(4,128)} %tile.41), slice={[0:3], [511:1310207]} | slice | bytes 31432704 | tf_op jit(solution)/shard_map/slice | solution.py:47
  92.4 44.4 %reshape.254 = f32[3929088]{0:T(1024)} reshape(f32[3,1309696]{1,0:T(4,128)} %slice.146) | data formatting | bytes 31432704
  136.8 24.7 %reshape.232 = f32[3,512,2558]{2,1,0:T(8,128)} reshape(f32[3929088]{0:T(1024)} %reshape.254) | data formatting | bytes 31432704 | tf_op jit(solution)/shard_map/reshape | solution.py:48
  169.1 24.2 %reshape.248 = f32[3938301]{0:T(1024)} reshape(f32[3,513,2559]{2,1,0:T(8,128)} %tile.42) | data formatting | bytes 31506408
  193.2 23.7 %tile.43 = f32[3,1312767]{1,0:T(4,128)} reshape(f32[3938301]{0:T(1024)} %reshape.248) | data formatting | bytes 31506408 | tf_op jit(solution)/shard_map/tile | solution.py:46
  217.0 21.6 %slice.149 = f32[3,1309696]{1,0:T(4,128)} slice(f32[3,1312767]{1,0:T(4,128)} %tile.43), slice={[0:3], [511:1310207]} | slice | bytes 31432704 | tf_op jit(solution)/shard_map/slice | solution.py:47
  238.5 44.7 %reshape.250 = f32[3929088]{0:T(1024)} reshape(f32[3,1309696]{1,0:T(4,128)} %slice.149) | data formatting | bytes 31432704
  283.2 24.8 %reshape.233 = f32[3,512,2558]{2,1,0:T(8,128)} reshape(f32[3929088]{0:T(1024)} %reshape.250) | data formatting | bytes 31432704 | tf_op jit(solution)/shard_map/reshape | solution.py:48
  315.5 23.9 %reshape.260 = f32[3938301]{0:T(1024)} reshape(f32[3,513,2559]{2,1,0:T(8,128)} %tile.16) | data formatting | bytes 31506408
  339.5 23.7 %tile.17 = f32[3,1312767]{1,0:T(4,128)} reshape(f32[3938301]{0:T(1024)} %reshape.260) | data formatting | bytes 31506408 | tf_op jit(solution)/shard_map/tile | solution.py:46
  363.2 21.8 %slice.140 = f32[3,1309696]{1,0:T(4,128)} slice(f32[3,1312767]{1,0:T(4,128)} %tile.17), slice={[0:3], [511:1310207]} | slice | bytes 31432704 | tf_op jit(solution)/shard_map/slice | solution.py:47
  385.0 44.4 %reshape.262 = f32[3929088]{0:T(1024)} reshape(f32[3,1309696]{1,0:T(4,128)} %slice.140) | data formatting | bytes 31432704
  429.5 24.8 %reshape.230 = f32[3,512,2558]{2,1,0:T(8,128)} reshape(f32[3929088]{0:T(1024)} %reshape.262) | data formatting | bytes 31432704 | tf_op jit(solution)/shard_map/reshape | solution.py:48
  461.8 24.2 %reshape.256 = f32[3938301]{0:T(1024)} reshape(f32[3,513,2559]{2,1,0:T(8,128)} %tile.18) | data formatting | bytes 31506408
  485.9 23.7 %tile.19 = f32[3,1312767]{1,0:T(4,128)} reshape(f32[3938301]{0:T(1024)} %reshape.256) | data formatting | bytes 31506408 | tf_op jit(solution)/shard_map/tile | solution.py:46
  509.7 21.6 %slice.143 = f32[3,1309696]{1,0:T(4,128)} slice(f32[3,1312767]{1,0:T(4,128)} %tile.19), slice={[0:3], [511:1310207]} | slice | bytes 31432704 | tf_op jit(solution)/shard_map/slice | solution.py:47
  531.3 44.7 %reshape.258 = f32[3929088]{0:T(1024)} reshape(f32[3,1309696]{1,0:T(4,128)} %slice.143) | data formatting | bytes 31432704
  575.9 24.8 %reshape.231 = f32[3,512,2558]{2,1,0:T(8,128)} reshape(f32[3929088]{0:T(1024)} %reshape.258) | data formatting | bytes 31432704 | tf_op jit(solution)/shard_map/reshape | solution.py:48
  600.7 19.4 slice_bitcast_fusion.7
  622.0 12.6 slice_bitcast_fusion.9
  635.3 34.5 %pad_maximum_fusion = f32[3,4,512,2048]{3,2,1,0:T(8,128)} fusion(f32[3,1,512,2048]{3,2,1,0:T(8,128)} %get-tuple-element.1597, f32[3,1,512,2048]{3,2,1,0:T(8,128)} %get-tuple-element.1598, f32[3,1,512,2048]{3,2,1,0:T(8,128)} %get-tuple-element.1599, f32[3,1,512,2048]{3,2,1,0:T(8,128)} %get-tuple-element.1600), kind=kLoop, calls=%fused_computation.120 | loop fusion | flops 37748736 | bytes 100663296 | tf_op jit(solution)/shard_map/stack | solution.py:58
  669.8 33.4 %slice_bitcast_fusion = (f32[4,512,2048]{2,1,0:T(8,128)}, f32[4,512,2048]{2,1,0:T(8,128)}, f32[4,512,2048]{2,1,0:T(8,128)}) fusion(f32[3,4,512,2048]{3,2,1,0:T(8,128)} %pad_maximum_fusion), kind=kLoop, calls=%fused_computation.122 | loop fusion | bytes 100663296 | tf_op jit(solution)/shard_map/squeeze | solution.py:212
  715.0 31.0 %while.109 = (s32[]{:T(128)}, bf16[2048,64]{0,1:T(8,128)(2,1)}, f32[2048]{0:T(1024)}, bf16[2048,64]{1,0:T(8,128)(2,1)}, bf16[2048,64]{1,0:T(8,128)(2,1)S(1)}, /*...) while((s32[]{:T(128)}, bf16[2048,64]{0,1:T(8,128)(2,1)}, ...), condition=%wide.region_8.9_spmd.clone, body=%wide.region_5.8_spmd.clone.sunk | while | flops 277939712 | bytes 17525440 | solution.py:88
  756.9 23.2 %while.108 = (s32[]{:T(128)}, bf16[2048,64]{0,1:T(8,128)(2,1)S(1)}, f32[2048]{0:T(1024)S(1)}, bf16[2048,64]{1,0:T(8,128)(2,1)}, bf16[2048,64]{1,0:T(8,128)(2,1)S...) while((s32[]{:T(128)}, bf16[2048,64]{0,1:T(8,128)(2,1)S(1)}, ...), condition=%wide.region_4.5_spmd.clone, body=%wide.region_1.4_spmd.clone.sunk | while | flops 277939712 | bytes 17787584 | solution.py:88
  792.2 27.5 %while.110 = (s32[]{:T(128)}, bf16[2048,64]{0,1:T(8,128)(2,1)S(1)}, f32[2048]{0:T(1024)S(1)}, bf16[2048,64]{1,0:T(8,128)(2,1)}, bf16[2048,64]{1,0:T(8,128)(2,1)S...) while((s32[]{:T(128)}, bf16[2048,64]{0,1:T(8,128)(2,1)S(1)}, ...), condition=%wide.region_12.13_spmd.clone, body=%wide.region_9.12_spmd.clone.sunk | while | flops 277939712 | bytes 17525440 | solution.py:88
  824.8 38.2 %reduce-scatter.5.cloned.1.call-done = bf16[512,768]{1,0:T(8,128)(2,1)} async-done(((bf16[2048,768]{1,0:T(8,128)(2,1)}), bf16[512,768]{1,0:T(8,128)(2,1)}) %reduce-scatter.5.cloned.1.call-update) | async-done | bytes 786448 | tf_op jit(solution)/shard_map/reduce_scatter | solution.py:220
  869.9 25.6 %all-gather.7.cloned.1.call-done = bf16[2048,768]{1,0:T(8,128)(2,1)} async-done(((bf16[512,768]{1,0:T(8,128)(2,1)}), bf16[2048,768]{1,0:T(8,128)(2,1)}) %all-gather.7.cloned.1.call-update) | async-done | bytes 3145744 | tf_op jit(solution)/shard_map/all_gather | solution.py:227
  909.7 38.0 %reduce-scatter.7.cloned.1.call-done = bf16[512,768]{1,0:T(8,128)(2,1)} async-done(((bf16[2048,768]{1,0:T(8,128)(2,1)}), bf16[512,768]{1,0:T(8,128)(2,1)}) %reduce-scatter.7.cloned.1.call-update) | async-done | bytes 786448 | tf_op jit(solution)/shard_map/reduce_scatter | solution.py:233
  950.5 28.6 %all-gather.9.cloned.1.call-done = bf16[2048,768]{1,0:T(8,128)(2,1)} async-done(((bf16[512,768]{1,0:T(8,128)(2,1)}), bf16[2048,768]{1,0:T(8,128)(2,1)}) %all-gather.9.cloned.1.call-update) | async-done | bytes 3145744 | tf_op jit(solution)/shard_map/all_gather | solution.py:243
  995.6 38.1 %reduce-scatter.9.cloned.1.call-done = bf16[512,768]{1,0:T(8,128)(2,1)} async-done(((bf16[2048,768]{1,0:T(8,128)(2,1)}), bf16[512,768]{1,0:T(8,128)(2,1)}) %reduce-scatter.9.cloned.1.call-update) | async-done | bytes 786448 | tf_op jit(solution)/shard_map/reduce_scatter | solution.py:260
  1038.9 28.6 %all-gather.11.cloned.1.call-done = bf16[2048,768]{1,0:T(8,128)(2,1)} async-done(((bf16[512,768]{1,0:T(8,128)(2,1)}), bf16[2048,768]{1,0:T(8,128)(2,1)}) %all-gather.11.cloned.1.call-update) | async-done | bytes 3145744 | tf_op jit(solution)/shard_map/all_gather | solution.py:271
  1080.0 76.9 %while.113 = (s32[]{:T(128)}, bf16[2048,64]{0,1:T(8,128)(2,1)}, f32[2048,64]{0,1:T(8,128)}, f32[2048,64]{0,1:T(8,128)S(1)}, f32[4,512,2048]{2,1,0:T(8,128)}, /*i...) while((s32[]{:T(128)}, bf16[2048,64]{0,1:T(8,128)(2,1)}, ...), condition=%wide.region_30.31_spmd.clone, body=%wide.region_28.30_spmd.clone.sunk | while | flops 684393984 | bytes 81214752 | solution.py:154
  1166.4 82.4 %while.112 = (s32[]{:T(128)}, bf16[2048,64]{0,1:T(8,128)(2,1)}, f32[2048,64]{0,1:T(8,128)}, f32[2048,64]{0,1:T(8,128)}, f32[4,512,2048]{2,1,0:T(8,128)}, /*index...) while((s32[]{:T(128)}, bf16[2048,64]{0,1:T(8,128)(2,1)}, ...), condition=%wide.region_27.28_spmd.clone, body=%wide.region_25.27_spmd.clone.sunk | while | flops 684393984 | bytes 80952608 | solution.py:154
  1257.5 77.5 %while.111 = (s32[]{:T(128)}, bf16[2048,64]{0,1:T(8,128)(2,1)}, f32[2048,64]{0,1:T(8,128)}, f32[2048,64]{0,1:T(8,128)}, f32[4,512,2048]{2,1,0:T(8,128)}, /*index...) while((s32[]{:T(128)}, bf16[2048,64]{0,1:T(8,128)(2,1)}, ...), condition=%wide.region_24.25_spmd.clone, body=%wide.region_22.24_spmd.clone.sunk | while | flops 684393984 | bytes 81214752 | solution.py:154
  1365.5 34.8 %pad_maximum_fusion.1 = f32[3,4,512,2048]{3,2,1,0:T(8,128)} fusion(f32[1,4,512,2048]{3,2,1,0:T(8,128)} %bitcast.176, f32[1,4,512,2048]{3,2,1,0:T(8,128)} %bitcast.177, f32[1,4,512,2048]{3,2,1,0:T(8,128)} %bitcast.175), kind=kLoop, calls=%fused_computation.121 | loop fusion | flops 25165824 | bytes 100663296 | tf_op jit(solution)/shard_map/stack | solution.py:305
  1400.3 32.0 %slice_bitcast_fusion.6 = (f32[3,512,2048]{2,1,0:T(8,128)}, f32[3,512,2048]{2,1,0:T(8,128)}, f32[3,512,2048]{2,1,0:T(8,128)}, f32[3,512,2048]{2,1,0:T(8,128)}) fusion(f32[3,4,512,2048]{3,2,1,0:T(8,128)} %pad_maximum_fusion.1), kind=kLoop, calls=%fused_computation.128 | loop fusion | bytes 100663296 | tf_op jit(solution)/shard_map/transpose(jvp())/unstack | solution.py:58
  1432.3 12.4 pad.36
  1444.8 25.4 %reshape.276 = f32[3929088]{0:T(1024)} reshape(f32[3,512,2558]{2,1,0:T(8,128)} %pad.36) | data formatting | bytes 31432704
  1470.1 22.6 %reshape.234 = f32[3,1309696]{1,0:T(4,128)} reshape(f32[3929088]{0:T(1024)} %reshape.276) | data formatting | bytes 31432704 | tf_op jit(solution)/shard_map/transpose(jvp())/reshape | solution.py:48
  1492.7 17.3 pad.37
  1510.0 47.6 %reshape.278 = f32[3938301]{0:T(1024)} reshape(f32[3,1312767]{1,0:T(4,128)} %pad.37) | data formatting | bytes 31506408
  1557.6 26.2 %reshape.235 = f32[3,513,2559]{2,1,0:T(8,128)} reshape(f32[3938301]{0:T(1024)} %reshape.278) | data formatting | bytes 31506408 | tf_op jit(solution)/shard_map/transpose(jvp())/reshape | solution.py:46
  1583.8 12.3 pad.39
  1596.2 25.6 %reshape.272 = f32[3929088]{0:T(1024)} reshape(f32[3,512,2558]{2,1,0:T(8,128)} %pad.39) | data formatting | bytes 31432704
  1621.8 22.5 %reshape.236 = f32[3,1309696]{1,0:T(4,128)} reshape(f32[3929088]{0:T(1024)} %reshape.272) | data formatting | bytes 31432704 | tf_op jit(solution)/shard_map/transpose(jvp())/reshape | solution.py:48
  1644.3 16.7 pad.40
  1661.0 46.3 %reshape.274 = f32[3938301]{0:T(1024)} reshape(f32[3,1312767]{1,0:T(4,128)} %pad.40) | data formatting | bytes 31506408
  1707.3 25.9 %reshape.237 = f32[3,513,2559]{2,1,0:T(8,128)} reshape(f32[3938301]{0:T(1024)} %reshape.274) | data formatting | bytes 31506408 | tf_op jit(solution)/shard_map/transpose(jvp())/reshape | solution.py:46
  1733.2 12.0 pad.42
  1745.2 25.3 %reshape.268 = f32[3929088]{0:T(1024)} reshape(f32[3,512,2558]{2,1,0:T(8,128)} %pad.42) | data formatting | bytes 31432704
  1770.5 22.5 %reshape.238 = f32[3,1309696]{1,0:T(4,128)} reshape(f32[3929088]{0:T(1024)} %reshape.268) | data formatting | bytes 31432704 | tf_op jit(solution)/shard_map/transpose(jvp())/reshape | solution.py:48
  1793.1 16.7 pad.43
  1809.8 46.5 %reshape.270 = f32[3938301]{0:T(1024)} reshape(f32[3,1312767]{1,0:T(4,128)} %pad.43) | data formatting | bytes 31506408
  1856.3 25.7 %reshape.239 = f32[3,513,2559]{2,1,0:T(8,128)} reshape(f32[3938301]{0:T(1024)} %reshape.270) | data formatting | bytes 31506408 | tf_op jit(solution)/shard_map/transpose(jvp())/reshape | solution.py:46
  1882.0 12.0 pad.45
  1894.0 25.3 %reshape.264 = f32[3929088]{0:T(1024)} reshape(f32[3,512,2558]{2,1,0:T(8,128)} %pad.45) | data formatting | bytes 31432704
  1919.2 22.5 %reshape.240 = f32[3,1309696]{1,0:T(4,128)} reshape(f32[3929088]{0:T(1024)} %reshape.264) | data formatting | bytes 31432704 | tf_op jit(solution)/shard_map/transpose(jvp())/reshape | solution.py:48
  1941.8 16.9 pad.46
  1958.7 46.3 %reshape.266 = f32[3938301]{0:T(1024)} reshape(f32[3,1312767]{1,0:T(4,128)} %pad.46) | data formatting | bytes 31506408
  2005.0 25.6 %reshape.241 = f32[3,513,2559]{2,1,0:T(8,128)} reshape(f32[3938301]{0:T(1024)} %reshape.266) | data formatting | bytes 31506408 | tf_op jit(solution)/shard_map/transpose(jvp())/reshape | solution.py:46
  2057.2 18.1 psum.68
  2077.4 44.5 %all-reduce.12 = (f32[]{:T(128)}, f32[]{:T(128)}, f32[768]{0:T(1024)S(1)}, f32[768]{0:T(1024)S(1)}) all-reduce(f32[]{:T(128)} %get-tuple-element.1419, f32[]{:T(128)} %fusion.150, f32[768]{0:T(1024)S(1)} %get-tuple-element.1420, f32[768]{0:T(1024)S(1)} %copy-done.64), channel_id=1, replica_groups=mesh['dp'=8,'tensor'=4] {'dp','tensor'}, use_global_device_ids=true, to_apply=%region_17.18 | all-reduce | flops 1538 | bytes 12304 | tf_op jit(solution)/shard_map/psum | solution.py:321
  (469 shorter events, 543.2 us)
Async XLA Ops:
  7.2 898.9 %copy-start = (bf16[512,768]{1,0:T(8,128)(2,1)S(1)}, bf16[512,768]{1,0:T(8,128)(2,1)}, u32[]{:S(2)}) copy-start(bf16[512,768]{1,0:T(8,128)(2,1)} %param.39) | copy-start | bytes 2359300
  7.2 696.0 %all-gather.5.cloned.1.call-start = ((), (), s32[]{:S(2)}) async-start(), calls=%async_computation.4 | async-start | bytes 3932160 | tf_op jit(solution)/shard_map/all_gather | solution.py:192
  12.8 850.2 %reduce-scatter.5.cloned.1.call-start = ((), (), s32[]{:S(2)}) async-start(), calls=%async_computation.5 | async-start | bytes 3932160 | tf_op jit(solution)/shard_map/reduce_scatter | solution.py:220
  429.5 24.8 %copy-start.46 = (f32[3,2559]{1,0:T(4,128)S(1)}, f32[3,2559]{1,0:T(4,128)}, u32[]{:S(2)}) copy-start(f32[3,2559]{1,0:T(4,128)} %get-tuple-element.1596) | copy-start | bytes 92128
  600.7 21.3 copy-start.15
  669.8 33.4 %copy-start.39 = (bf16[768,192]{0,1:T(8,128)(2,1)S(1)}, bf16[768,192]{0,1:T(8,128)(2,1)}, u32[]{:S(2)}) copy-start(bf16[768,192]{0,1:T(8,128)(2,1)} %param.31) | copy-start | bytes 884740
  746.0 7.3 copy-start.20
  780.6 7.3 copy-start.9
  780.6 7.3 copy-start.18
  820.7 42.3 %copy-start.13 = (bf16[512,768]{1,0:T(8,128)(2,1)S(1)}, bf16[512,768]{1,0:T(8,128)(2,1)}, u32[]{:S(2)}) copy-start(bf16[512,768]{1,0:T(8,128)(2,1)} %param.26) | copy-start | bytes 2359300
  824.7 70.8 %all-gather.7.cloned.1.call-start = ((), (), s32[]{:S(2)}) async-start(), calls=%async_computation.6 | async-start | bytes 3932160 | tf_op jit(solution)/shard_map/all_gather | solution.py:227
  824.8 42.1 %copy-start.37 = (bf16[768,512]{1,0:T(8,128)(2,1)S(1)}, bf16[768,512]{1,0:T(8,128)(2,1)}, u32[]{:S(2)}) copy-start(bf16[768,512]{1,0:T(8,128)(2,1)} %param.37) | copy-start | bytes 2359300
  824.8 212.2 %copy-start.47 = (f32[768]{0:T(1024)}, f32[768]{0:T(1024)S(1)}, u32[]{:S(2)}) copy-start(f32[768]{0:T(1024)S(1)} %convert_element_type.265) | copy-start | bytes 9220
  864.5 172.5 %copy-start.53 = (f32[512]{0:T(512)}, f32[512]{0:T(512)S(1)}, u32[]{:S(2)}) copy-start(f32[512]{0:T(512)S(1)} %fusion.149) | copy-start | bytes 6148
  866.8 80.9 %reduce-scatter.7.cloned.1.call-start = ((), (), s32[]{:S(2)}) async-start(), calls=%async_computation.7 | async-start | bytes 3932160 | tf_op jit(solution)/shard_map/reduce_scatter | solution.py:233
  906.1 41.7 %copy-start.16 = (bf16[512,768]{1,0:T(8,128)(2,1)S(1)}, bf16[512,768]{1,0:T(8,128)(2,1)}, u32[]{:S(2)}) copy-start(bf16[512,768]{1,0:T(8,128)(2,1)} %reduce-scatter.5.cloned.1.call-done) | copy-start | bytes 2359300
  909.6 69.5 %all-gather.9.cloned.1.call-start = ((), (), s32[]{:S(2)}) async-start(), calls=%async_computation.8 | async-start | bytes 3932160 | tf_op jit(solution)/shard_map/all_gather | solution.py:243
  909.7 127.3 %copy-start.51 = (f32[512]{0:T(512)}, f32[512]{0:T(512)S(1)}, u32[]{:S(2)}) copy-start(f32[512]{0:T(512)S(1)} %fusion.147) | copy-start | bytes 6148
  950.5 83.2 %reduce-scatter.9.cloned.1.call-start = ((), (), s32[]{:S(2)}) async-start(), calls=%async_computation.9 | async-start | bytes 3932160 | tf_op jit(solution)/shard_map/reduce_scatter | solution.py:260
  989.1 44.6 %copy-start.24 = (bf16[512,768]{1,0:T(8,128)(2,1)S(1)}, bf16[512,768]{1,0:T(8,128)(2,1)}, u32[]{:S(2)}) copy-start(bf16[512,768]{1,0:T(8,128)(2,1)} %param.27) | copy-start | bytes 2359300
  995.6 71.9 %copy-start.45 = (bf16[192,768]{1,0:T(8,128)(2,1)S(1)}, bf16[192,768]{1,0:T(8,128)(2,1)}, u32[]{:S(2)}) copy-start(bf16[192,768]{1,0:T(8,128)(2,1)} %param.34) | copy-start | bytes 884740
  995.6 71.9 %all-gather.11.cloned.1.call-start = ((), (), s32[]{:S(2)}) async-start(), calls=%async_computation.10 | async-start | bytes 3932160 | tf_op jit(solution)/shard_map/all_gather | solution.py:271
  1037.0 33.5 %copy-start.62 = (f32[512]{0:T(512)}, f32[512]{0:T(512)S(1)}, u32[]{:S(2)}) copy-start(f32[512]{0:T(512)S(1)} %multiply_multiply_fusion.4) | copy-start | bytes 6148
  1038.8 1036.6 %reduce-scatter.11.cloned.1.call-start = ((), (), s32[]{:S(2)}) async-start(), calls=%async_computation.11 | async-start | bytes 3932160 | tf_op jit(solution)/shard_map/reduce_scatter | solution.py:310
  1086.7 7.3 copy-start.2
  1105.7 7.4 copy-start.2
  1125.0 7.3 copy-start.2
  1144.2 7.3 copy-start.2
  1157.7 8.7 copy-start.12
  1157.7 8.7 copy-start.21
  1173.3 7.3 copy-start.4
  1193.4 7.3 copy-start.4
  1214.0 7.4 copy-start.4
  1234.6 7.3 copy-start.4
  1248.8 8.7 copy-start.10
  1248.8 8.7 copy-start.19
  1263.5 7.3 copy-start.6
  1282.0 7.3 copy-start.6
  1301.7 7.4 copy-start.6
  1321.4 7.3 copy-start.6
  1335.0 8.4 copy-start.23
  1335.0 9.9 copy-start.40
  1335.0 9.9 copy-start.42
  1335.1 9.9 copy-start.44
  1349.0 779.6 %all-reduce.16.cloned.1.call-start = ((), (), s32[]{:S(2)}) async-start(), calls=%async_computation.12 | async-start | bytes 14155776 | tf_op jit(solution)/shard_map/psum | solution.py:324
  1349.3 5.0 copy-start.66
  1349.3 5.0 copy-start.69
  1349.3 5.0 copy-start.71
  1354.3 5.1 copy-start.30
  1354.3 5.1 copy-start.32
  1354.3 6.7 copy-start.59
  2049.9 6.7 copy-start.67
  2049.9 25.5 %copy-start.14 = (bf16[512,768]{1,0:T(8,128)(2,1)S(1)}, bf16[512,768]{1,0:T(8,128)(2,1)}, u32[]{:S(2)}) copy-start(bf16[512,768]{1,0:T(8,128)(2,1)} %param.26) | copy-start | bytes 2359300
  2049.9 25.5 %copy-start.50 = (f32[768]{0:T(1024)S(1)}, f32[768]{0:T(1024)}, u32[]{:S(2)}) copy-start(f32[768]{0:T(1024)} %copy-done.49) | copy-start | bytes 9220
  2049.9 25.5 %copy-start.57 = (f32[512]{0:T(512)S(1)}, f32[512]{0:T(512)}, u32[]{:S(2)}) copy-start(f32[512]{0:T(512)} %copy-done.56) | copy-start | bytes 6148
  2049.9 27.4 %copy-start.64 = (f32[768]{0:T(1024)S(1)}, f32[768]{0:T(1024)}, u32[]{:S(2)}) copy-start(f32[768]{0:T(1024)} %get-tuple-element.1417) | copy-start | bytes 9220
  2049.9 73.9 %copy-start.61 = (f32[512]{0:T(512)S(1)}, f32[512]{0:T(512)}, u32[]{:S(2)}) copy-start(f32[512]{0:T(512)} %copy-done.60) | copy-start | bytes 6148
  2049.9 75.1 %copy-start.17 = (bf16[512,768]{1,0:T(8,128)(2,1)S(1)}, bf16[512,768]{1,0:T(8,128)(2,1)}, u32[]{:S(2)}) copy-start(bf16[512,768]{1,0:T(8,128)(2,1)} %reduce-scatter.5.cloned.1.call-done) | copy-start | bytes 2359300
  2049.9 75.1 %copy-start.25 = (bf16[512,768]{1,0:T(8,128)(2,1)S(1)}, bf16[512,768]{1,0:T(8,128)(2,1)}, u32[]{:S(2)}) copy-start(bf16[512,768]{1,0:T(8,128)(2,1)} %param.27) | copy-start | bytes 2359300
  2050.0 75.1 %copy-start.27 = (bf16[512,768]{1,0:T(8,128)(2,1)S(1)}, bf16[512,768]{1,0:T(8,128)(2,1)}, u32[]{:S(2)}) copy-start(bf16[512,768]{1,0:T(8,128)(2,1)} %reduce-scatter.7.cloned.1.call-done) | copy-start | bytes 2359300
  2050.0 75.1 %copy-start.48 = (f32[768]{0:T(1024)S(1)}, f32[768]{0:T(1024)}, u32[]{:S(2)}) copy-start(f32[768]{0:T(1024)} %copy-done.47) | copy-start | bytes 9220
  2050.0 75.1 %copy-start.52 = (f32[512]{0:T(512)S(1)}, f32[512]{0:T(512)}, u32[]{:S(2)}) copy-start(f32[512]{0:T(512)} %copy-done.51) | copy-start | bytes 6148
  2050.0 75.1 %copy-start.54 = (f32[512]{0:T(512)S(1)}, f32[512]{0:T(512)}, u32[]{:S(2)}) copy-start(f32[512]{0:T(512)} %copy-done.53) | copy-start | bytes 6148
  2050.0 75.1 %copy-start.63 = (f32[512]{0:T(512)S(1)}, f32[512]{0:T(512)}, u32[]{:S(2)}) copy-start(f32[512]{0:T(512)} %copy-done.62) | copy-start | bytes 6148
  (35 other events, 108.5 us)
Sparse Core Ops, SparseCore 0:
  12.9 28.7 all-gather.4
  824.8 38.1 reduce-scatter.4
  866.9 28.5 all-gather.6
  909.8 37.9 reduce-scatter.6
  950.6 28.5 all-gather.8
  995.7 37.9 reduce-scatter.8
  1038.9 28.5 all-gather.10
  1349.2 37.9 reduce-scatter.10
  1392.8 235.1 all-reduce.15
where the time goes:
time: 2160 us; the launch traced here: 2140 us
  local copies, waits for them, and re-layouts  1340 us (62%)
  matrix products  269 us (12%)
  other arithmetic  252 us (12%)
  waiting for transfers between devices  197 us (9%)
  blocking collectives  62.7 us (3%)
    unnamed x163, local copies, waits for them, and re-layouts  585 us
    reshape x8, local copies, waits for them, and re-layouts, band_matrix(): return tiled.reshape(heads_here, block_rows, span - 1)[:, :, :seq_len]  189 us
    another operation x8, local copies, waits for them, and re-layouts, band_matrix(): tiled = jnp.tile(window, (1, block_rows + 1))  126 us
    reshape x4, local copies, waits for them, and re-layouts, band_matrix(): tiled = jnp.tile(window, (1, block_rows + 1))  103 us
    dynamic_update_slice x12, other arithmetic, one_block(): lax.dynamic_update_slice_in_dim(grad_band, current + grad_scores.astype(j...  88.1 us
    slice x4, local copies, waits for them, and re-layouts, band_matrix(): tiled = tiled[:, block_rows - 1:block_rows - 1 + block_rows * (span - 1)]  86.8 us
    dot_general x24, matrix products, one_block(): lax.dot_general(query_block, key_head, contract_cols, preferred_element_t...  84 us
    pad x4, local copies, waits for them, and re-layouts, band_matrix(): tiled = tiled[:, block_rows - 1:block_rows - 1 + block_rows * (span - 1)]  67.5 us
  transfers between devices with their start and end apart: 9, of which 6 were waited for; matrix products, arithmetic and copies ran while one was open for 66% of the time, Pallas kernels for 0%

commit v1 on v0

--- a/solution.py
+++ b/solution.py
@@ -319,7 +319,7 @@
     grad_source_part, grad_gain_attn = norm_back_attn(grad_normed)
     grad_source = grad_middle + grad_source_part
     gain_attn_total, gain_ff_total, loss_total, count_total = lax.psum(
-        (grad_gain_attn, grad_gain_ff, loss_part, count_part), ("dp", "tensor")
+        lax.psum((grad_gain_attn, grad_gain_ff, loss_part, count_part), "dp"), "tensor"
     )
     grad_w_joint, grad_out, grad_table, grad_w_pair, grad_down = lax.psum(
         (grad_w_joint, grad_out, grad_table, grad_w_pair, grad_down), "dp"

time: 2160 us -> 2140 us (level)
  blocking collectives: 62.7 us -> 41 us
    psum x2, blocking collectives: 62.7 us -> 41 us  [the longest x1 33.9 us: on_device(): lax.psum((grad_gain_attn, grad_gain_ff, loss_part, count_part), 'dp')]
where the time goes in v1:
time: 2140 us; the launch traced here: 2120 us
  local copies, waits for them, and re-layouts  1340 us (63%)
  matrix products  269 us (13%)
  other arithmetic  251 us (12%)
  waiting for transfers between devices  197 us (9%)
  blocking collectives  41 us (2%)
    unnamed x163, local copies, waits for them, and re-layouts  585 us
    reshape x8, local copies, waits for them, and re-layouts, band_matrix(): return tiled.reshape(heads_here, block_rows, span - 1)[:, :, :seq_len]  189 us
    another operation x8, local copies, waits for them, and re-layouts, band_matrix(): tiled = jnp.tile(window, (1, block_rows + 1))  126 us
    reshape x4, local copies, waits for them, and re-layouts, band_matrix(): tiled = jnp.tile(window, (1, block_rows + 1))  103 us
    dynamic_update_slice x12, other arithmetic, one_block(): lax.dynamic_update_slice_in_dim(grad_band, current + grad_scores.astype(j...  88.1 us
    slice x4, local copies, waits for them, and re-layouts, band_matrix(): tiled = tiled[:, block_rows - 1:block_rows - 1 + block_rows * (span - 1)]  86.8 us
    dot_general x24, matrix products, one_block(): lax.dot_general(query_block, key_head, contract_cols, preferred_element_t...  84 us
    pad x4, local copies, waits for them, and re-layouts, band_matrix(): tiled = tiled[:, block_rows - 1:block_rows - 1 + block_rows * (span - 1)]  67.5 us
  transfers between devices with their start and end apart: 9, of which 6 were waited for; matrix products, arithmetic and copies ran while one was open for 66% of the time, Pallas kernels for 0%

profile of v1, /device:TPU:12, one launch (start us, length us, event | category | flops | bytes accessed | tf_op | source)
XLA Modules:
  0.0 2122.2 jit_solution(13337127635505050100)
XLA Ops:
  14.5 8.1 tile.40
  22.7 24.2 %reshape.252 = f32[3938301]{0:T(1024)} reshape(f32[3,513,2559]{2,1,0:T(8,128)} %tile.40) | data formatting | bytes 31506408
  46.9 23.7 %tile.41 = f32[3,1312767]{1,0:T(4,128)} reshape(f32[3938301]{0:T(1024)} %reshape.252) | data formatting | bytes 31506408 | tf_op jit(solution)/shard_map/tile | solution.py:46
  70.6 21.8 %slice.146 = f32[3,1309696]{1,0:T(4,128)} slice(f32[3,1312767]{1,0:T(4,128)} %tile.41), slice={[0:3], [511:1310207]} | slice | bytes 31432704 | tf_op jit(solution)/shard_map/slice | solution.py:47
  92.4 44.4 %reshape.254 = f32[3929088]{0:T(1024)} reshape(f32[3,1309696]{1,0:T(4,128)} %slice.146) | data formatting | bytes 31432704
  136.9 24.7 %reshape.232 = f32[3,512,2558]{2,1,0:T(8,128)} reshape(f32[3929088]{0:T(1024)} %reshape.254) | data formatting | bytes 31432704 | tf_op jit(solution)/shard_map/reshape | solution.py:48
  169.1 24.2 %reshape.248 = f32[3938301]{0:T(1024)} reshape(f32[3,513,2559]{2,1,0:T(8,128)} %tile.42) | data formatting | bytes 31506408
  193.3 23.7 %tile.43 = f32[3,1312767]{1,0:T(4,128)} reshape(f32[3938301]{0:T(1024)} %reshape.248) | data formatting | bytes 31506408 | tf_op jit(solution)/shard_map/tile | solution.py:46
  217.0 21.6 %slice.149 = f32[3,1309696]{1,0:T(4,128)} slice(f32[3,1312767]{1,0:T(4,128)} %tile.43), slice={[0:3], [511:1310207]} | slice | bytes 31432704 | tf_op jit(solution)/shard_map/slice | solution.py:47
  238.6 44.6 %reshape.250 = f32[3929088]{0:T(1024)} reshape(f32[3,1309696]{1,0:T(4,128)} %slice.149) | data formatting | bytes 31432704
  283.2 24.8 %reshape.233 = f32[3,512,2558]{2,1,0:T(8,128)} reshape(f32[3929088]{0:T(1024)} %reshape.250) | data formatting | bytes 31432704 | tf_op jit(solution)/shard_map/reshape | solution.py:48
  315.6 23.9 %reshape.260 = f32[3938301]{0:T(1024)} reshape(f32[3,513,2559]{2,1,0:T(8,128)} %tile.16) | data formatting | bytes 31506408
  339.5 23.7 %tile.17 = f32[3,1312767]{1,0:T(4,128)} reshape(f32[3938301]{0:T(1024)} %reshape.260) | data formatting | bytes 31506408 | tf_op jit(solution)/shard_map/tile | solution.py:46
  363.3 21.8 %slice.140 = f32[3,1309696]{1,0:T(4,128)} slice(f32[3,1312767]{1,0:T(4,128)} %tile.17), slice={[0:3], [511:1310207]} | slice | bytes 31432704 | tf_op jit(solution)/shard_map/slice | solution.py:47
  385.1 44.4 %reshape.262 = f32[3929088]{0:T(1024)} reshape(f32[3,1309696]{1,0:T(4,128)} %slice.140) | data formatting | bytes 31432704
  429.5 24.8 %reshape.230 = f32[3,512,2558]{2,1,0:T(8,128)} reshape(f32[3929088]{0:T(1024)} %reshape.262) | data formatting | bytes 31432704 | tf_op jit(solution)/shard_map/reshape | solution.py:48
  461.8 24.2 %reshape.256 = f32[3938301]{0:T(1024)} reshape(f32[3,513,2559]{2,1,0:T(8,128)} %tile.18) | data formatting | bytes 31506408
  486.0 23.7 %tile.19 = f32[3,1312767]{1,0:T(4,128)} reshape(f32[3938301]{0:T(1024)} %reshape.256) | data formatting | bytes 31506408 | tf_op jit(solution)/shard_map/tile | solution.py:46
  509.7 21.6 %slice.143 = f32[3,1309696]{1,0:T(4,128)} slice(f32[3,1312767]{1,0:T(4,128)} %tile.19), slice={[0:3], [511:1310207]} | slice | bytes 31432704 | tf_op jit(solution)/shard_map/slice | solution.py:47
  531.3 44.7 %reshape.258 = f32[3929088]{0:T(1024)} reshape(f32[3,1309696]{1,0:T(4,128)} %slice.143) | data formatting | bytes 31432704
  576.0 24.8 %reshape.231 = f32[3,512,2558]{2,1,0:T(8,128)} reshape(f32[3929088]{0:T(1024)} %reshape.258) | data formatting | bytes 31432704 | tf_op jit(solution)/shard_map/reshape | solution.py:48
  600.8 19.4 slice_bitcast_fusion.7
  622.1 12.6 slice_bitcast_fusion.9
  635.4 34.5 %pad_maximum_fusion = f32[3,4,512,2048]{3,2,1,0:T(8,128)} fusion(f32[3,1,512,2048]{3,2,1,0:T(8,128)} %get-tuple-element.1602, f32[3,1,512,2048]{3,2,1,0:T(8,128)} %get-tuple-element.1603, f32[3,1,512,2048]{3,2,1,0:T(8,128)} %get-tuple-element.1604, f32[3,1,512,2048]{3,2,1,0:T(8,128)} %get-tuple-element.1605), kind=kLoop, calls=%fused_computation.120 | loop fusion | flops 37748736 | bytes 100663296 | tf_op jit(solution)/shard_map/stack | solution.py:58
  669.9 33.4 %slice_bitcast_fusion = (f32[4,512,2048]{2,1,0:T(8,128)}, f32[4,512,2048]{2,1,0:T(8,128)}, f32[4,512,2048]{2,1,0:T(8,128)}) fusion(f32[3,4,512,2048]{3,2,1,0:T(8,128)} %pad_maximum_fusion), kind=kLoop, calls=%fused_computation.122 | loop fusion | bytes 100663296 | tf_op jit(solution)/shard_map/squeeze | solution.py:212
  715.1 31.0 %while.109 = (s32[]{:T(128)}, bf16[2048,64]{0,1:T(8,128)(2,1)}, f32[2048]{0:T(1024)}, bf16[2048,64]{1,0:T(8,128)(2,1)}, bf16[2048,64]{1,0:T(8,128)(2,1)S(1)}, /*...) while((s32[]{:T(128)}, bf16[2048,64]{0,1:T(8,128)(2,1)}, ...), condition=%wide.region_8.9_spmd.clone, body=%wide.region_5.8_spmd.clone.sunk | while | flops 277939712 | bytes 17525440 | solution.py:88
  756.9 23.2 %while.108 = (s32[]{:T(128)}, bf16[2048,64]{0,1:T(8,128)(2,1)S(1)}, f32[2048]{0:T(1024)S(1)}, bf16[2048,64]{1,0:T(8,128)(2,1)}, bf16[2048,64]{1,0:T(8,128)(2,1)S...) while((s32[]{:T(128)}, bf16[2048,64]{0,1:T(8,128)(2,1)S(1)}, ...), condition=%wide.region_4.5_spmd.clone, body=%wide.region_1.4_spmd.clone.sunk | while | flops 277939712 | bytes 17787584 | solution.py:88
  792.3 27.5 %while.110 = (s32[]{:T(128)}, bf16[2048,64]{0,1:T(8,128)(2,1)S(1)}, f32[2048]{0:T(1024)S(1)}, bf16[2048,64]{1,0:T(8,128)(2,1)}, bf16[2048,64]{1,0:T(8,128)(2,1)S...) while((s32[]{:T(128)}, bf16[2048,64]{0,1:T(8,128)(2,1)S(1)}, ...), condition=%wide.region_12.13_spmd.clone, body=%wide.region_9.12_spmd.clone.sunk | while | flops 277939712 | bytes 17525440 | solution.py:88
  824.9 38.2 %reduce-scatter.5.cloned.1.call-done = bf16[512,768]{1,0:T(8,128)(2,1)} async-done(((bf16[2048,768]{1,0:T(8,128)(2,1)}), bf16[512,768]{1,0:T(8,128)(2,1)}) %reduce-scatter.5.cloned.1.call-update) | async-done | bytes 786448 | tf_op jit(solution)/shard_map/reduce_scatter | solution.py:220
  870.0 25.6 %all-gather.7.cloned.1.call-done = bf16[2048,768]{1,0:T(8,128)(2,1)} async-done(((bf16[512,768]{1,0:T(8,128)(2,1)}), bf16[2048,768]{1,0:T(8,128)(2,1)}) %all-gather.7.cloned.1.call-update) | async-done | bytes 3145744 | tf_op jit(solution)/shard_map/all_gather | solution.py:227
  909.8 38.0 %reduce-scatter.7.cloned.1.call-done = bf16[512,768]{1,0:T(8,128)(2,1)} async-done(((bf16[2048,768]{1,0:T(8,128)(2,1)}), bf16[512,768]{1,0:T(8,128)(2,1)}) %reduce-scatter.7.cloned.1.call-update) | async-done | bytes 786448 | tf_op jit(solution)/shard_map/reduce_scatter | solution.py:233
  950.6 28.6 %all-gather.9.cloned.1.call-done = bf16[2048,768]{1,0:T(8,128)(2,1)} async-done(((bf16[512,768]{1,0:T(8,128)(2,1)}), bf16[2048,768]{1,0:T(8,128)(2,1)}) %all-gather.9.cloned.1.call-update) | async-done | bytes 3145744 | tf_op jit(solution)/shard_map/all_gather | solution.py:243
  995.7 38.1 %reduce-scatter.9.cloned.1.call-done = bf16[512,768]{1,0:T(8,128)(2,1)} async-done(((bf16[2048,768]{1,0:T(8,128)(2,1)}), bf16[512,768]{1,0:T(8,128)(2,1)}) %reduce-scatter.9.cloned.1.call-update) | async-done | bytes 786448 | tf_op jit(solution)/shard_map/reduce_scatter | solution.py:260
  1039.0 28.6 %all-gather.11.cloned.1.call-done = bf16[2048,768]{1,0:T(8,128)(2,1)} async-done(((bf16[512,768]{1,0:T(8,128)(2,1)}), bf16[2048,768]{1,0:T(8,128)(2,1)}) %all-gather.11.cloned.1.call-update) | async-done | bytes 3145744 | tf_op jit(solution)/shard_map/all_gather | solution.py:271
  1080.1 77.0 %while.113 = (s32[]{:T(128)}, bf16[2048,64]{0,1:T(8,128)(2,1)}, f32[2048,64]{0,1:T(8,128)}, f32[2048,64]{0,1:T(8,128)S(1)}, f32[4,512,2048]{2,1,0:T(8,128)}, /*i...) while((s32[]{:T(128)}, bf16[2048,64]{0,1:T(8,128)(2,1)}, ...), condition=%wide.region_32.33_spmd.clone, body=%wide.region_30.32_spmd.clone.sunk | while | flops 684393984 | bytes 81214752 | solution.py:154
  1166.6 82.4 %while.112 = (s32[]{:T(128)}, bf16[2048,64]{0,1:T(8,128)(2,1)}, f32[2048,64]{0,1:T(8,128)}, f32[2048,64]{0,1:T(8,128)}, f32[4,512,2048]{2,1,0:T(8,128)}, /*index...) while((s32[]{:T(128)}, bf16[2048,64]{0,1:T(8,128)(2,1)}, ...), condition=%wide.region_29.30_spmd.clone, body=%wide.region_27.29_spmd.clone.sunk | while | flops 684393984 | bytes 80952608 | solution.py:154
  1257.7 77.6 %while.111 = (s32[]{:T(128)}, bf16[2048,64]{0,1:T(8,128)(2,1)}, f32[2048,64]{0,1:T(8,128)}, f32[2048,64]{0,1:T(8,128)}, f32[4,512,2048]{2,1,0:T(8,128)}, /*index...) while((s32[]{:T(128)}, bf16[2048,64]{0,1:T(8,128)(2,1)}, ...), condition=%wide.region_26.27_spmd.clone, body=%wide.region_24.26_spmd.clone.sunk | while | flops 684393984 | bytes 81214752 | solution.py:154
  1365.7 34.6 %pad_maximum_fusion.1 = f32[3,4,512,2048]{3,2,1,0:T(8,128)} fusion(f32[1,4,512,2048]{3,2,1,0:T(8,128)} %bitcast.176, f32[1,4,512,2048]{3,2,1,0:T(8,128)} %bitcast.177, f32[1,4,512,2048]{3,2,1,0:T(8,128)} %bitcast.175), kind=kLoop, calls=%fused_computation.121 | loop fusion | flops 25165824 | bytes 100663296 | tf_op jit(solution)/shard_map/stack | solution.py:305
  1400.4 32.0 %slice_bitcast_fusion.6 = (f32[3,512,2048]{2,1,0:T(8,128)}, f32[3,512,2048]{2,1,0:T(8,128)}, f32[3,512,2048]{2,1,0:T(8,128)}, f32[3,512,2048]{2,1,0:T(8,128)}) fusion(f32[3,4,512,2048]{3,2,1,0:T(8,128)} %pad_maximum_fusion.1), kind=kLoop, calls=%fused_computation.128 | loop fusion | bytes 100663296 | tf_op jit(solution)/shard_map/transpose(jvp())/unstack | solution.py:58
  1432.4 12.4 pad.36
  1444.8 25.4 %reshape.276 = f32[3929088]{0:T(1024)} reshape(f32[3,512,2558]{2,1,0:T(8,128)} %pad.36) | data formatting | bytes 31432704
  1470.2 22.6 %reshape.234 = f32[3,1309696]{1,0:T(4,128)} reshape(f32[3929088]{0:T(1024)} %reshape.276) | data formatting | bytes 31432704 | tf_op jit(solution)/shard_map/transpose(jvp())/reshape | solution.py:48
  1492.8 17.3 pad.37
  1510.1 47.7 %reshape.278 = f32[3938301]{0:T(1024)} reshape(f32[3,1312767]{1,0:T(4,128)} %pad.37) | data formatting | bytes 31506408
  1557.7 26.2 %reshape.235 = f32[3,513,2559]{2,1,0:T(8,128)} reshape(f32[3938301]{0:T(1024)} %reshape.278) | data formatting | bytes 31506408 | tf_op jit(solution)/shard_map/transpose(jvp())/reshape | solution.py:46
  1583.9 12.3 pad.39
  1596.3 25.6 %reshape.272 = f32[3929088]{0:T(1024)} reshape(f32[3,512,2558]{2,1,0:T(8,128)} %pad.39) | data formatting | bytes 31432704
  1621.9 22.6 %reshape.236 = f32[3,1309696]{1,0:T(4,128)} reshape(f32[3929088]{0:T(1024)} %reshape.272) | data formatting | bytes 31432704 | tf_op jit(solution)/shard_map/transpose(jvp())/reshape | solution.py:48
  1644.4 16.7 pad.40
  1661.1 46.3 %reshape.274 = f32[3938301]{0:T(1024)} reshape(f32[3,1312767]{1,0:T(4,128)} %pad.40) | data formatting | bytes 31506408
  1707.5 25.9 %reshape.237 = f32[3,513,2559]{2,1,0:T(8,128)} reshape(f32[3938301]{0:T(1024)} %reshape.274) | data formatting | bytes 31506408 | tf_op jit(solution)/shard_map/transpose(jvp())/reshape | solution.py:46
  1733.3 12.0 pad.42
  1745.3 25.3 %reshape.268 = f32[3929088]{0:T(1024)} reshape(f32[3,512,2558]{2,1,0:T(8,128)} %pad.42) | data formatting | bytes 31432704
  1770.7 22.6 %reshape.238 = f32[3,1309696]{1,0:T(4,128)} reshape(f32[3929088]{0:T(1024)} %reshape.268) | data formatting | bytes 31432704 | tf_op jit(solution)/shard_map/transpose(jvp())/reshape | solution.py:48
  1793.2 16.7 pad.43
  1809.9 46.5 %reshape.270 = f32[3938301]{0:T(1024)} reshape(f32[3,1312767]{1,0:T(4,128)} %pad.43) | data formatting | bytes 31506408
  1856.5 25.7 %reshape.239 = f32[3,513,2559]{2,1,0:T(8,128)} reshape(f32[3938301]{0:T(1024)} %reshape.270) | data formatting | bytes 31506408 | tf_op jit(solution)/shard_map/transpose(jvp())/reshape | solution.py:46
  1882.1 12.0 pad.45
  1894.2 25.2 %reshape.264 = f32[3929088]{0:T(1024)} reshape(f32[3,512,2558]{2,1,0:T(8,128)} %pad.45) | data formatting | bytes 31432704
  1919.4 22.6 %reshape.240 = f32[3,1309696]{1,0:T(4,128)} reshape(f32[3929088]{0:T(1024)} %reshape.264) | data formatting | bytes 31432704 | tf_op jit(solution)/shard_map/transpose(jvp())/reshape | solution.py:48
  1942.0 16.9 pad.46
  1958.9 46.3 %reshape.266 = f32[3938301]{0:T(1024)} reshape(f32[3,1312767]{1,0:T(4,128)} %pad.46) | data formatting | bytes 31506408
  2005.2 25.6 %reshape.241 = f32[3,513,2559]{2,1,0:T(8,128)} reshape(f32[3938301]{0:T(1024)} %reshape.266) | data formatting | bytes 31506408 | tf_op jit(solution)/shard_map/transpose(jvp())/reshape | solution.py:46
  2059.4 33.9 %all-reduce.12 = (f32[]{:T(128)}, f32[]{:T(128)}, f32[768]{0:T(1024)S(1)}, f32[32,3]{0,1:T(4,128)S(1)}, f32[768]{0:T(1024)S(1)}) all-reduce(f32[]{:T(128)} %get-tuple-element.1419, f32[]{:T(128)} %fusion.150, f32[768]{0:T(1024)S(1)} %get-tuple-element.1420, f32[32,3]{0,1:T(4,128)S(1)} %fusion.115, ...), channel_id=1, replica_groups=mesh['dp'=8,'tensor'=4] {'dp'}, use_global_device_ids=true, to_apply=%region_17.18 | all-reduce | flops 1634 | bytes 13072 | tf_op jit(solution)/shard_map/psum | solution.py:322
  (469 shorter events, 542.2 us)
Async XLA Ops:
  7.2 899.0 %copy-start = (bf16[512,768]{1,0:T(8,128)(2,1)S(1)}, bf16[512,768]{1,0:T(8,128)(2,1)}, u32[]{:S(2)}) copy-start(bf16[512,768]{1,0:T(8,128)(2,1)} %param.39) | copy-start | bytes 2359300
  7.2 696.1 %all-gather.5.cloned.1.call-start = ((), (), s32[]{:S(2)}) async-start(), calls=%async_computation.4 | async-start | bytes 3932160 | tf_op jit(solution)/shard_map/all_gather | solution.py:192
  12.8 850.3 %reduce-scatter.5.cloned.1.call-start = ((), (), s32[]{:S(2)}) async-start(), calls=%async_computation.5 | async-start | bytes 3932160 | tf_op jit(solution)/shard_map/reduce_scatter | solution.py:220
  429.5 24.8 %copy-start.46 = (f32[3,2559]{1,0:T(4,128)S(1)}, f32[3,2559]{1,0:T(4,128)}, u32[]{:S(2)}) copy-start(f32[3,2559]{1,0:T(4,128)} %get-tuple-element.1601) | copy-start | bytes 92128
  600.8 21.3 %copy-start.15 = (f32[3,512,2558]{2,1,0:T(8,128)S(1)}, f32[3,512,2558]{2,1,0:T(8,128)}, u32[]{:S(2)}) copy-start(f32[3,512,2558]{2,1,0:T(8,128)} %reshape.231) | copy-start | bytes 47149060
  669.9 33.4 %copy-start.39 = (bf16[768,192]{0,1:T(8,128)(2,1)S(1)}, bf16[768,192]{0,1:T(8,128)(2,1)}, u32[]{:S(2)}) copy-start(bf16[768,192]{0,1:T(8,128)(2,1)} %param.31) | copy-start | bytes 884740
  746.1 7.3 copy-start.20
  780.7 7.3 copy-start.9
  780.7 7.3 copy-start.18
  820.8 42.3 %copy-start.13 = (bf16[512,768]{1,0:T(8,128)(2,1)S(1)}, bf16[512,768]{1,0:T(8,128)(2,1)}, u32[]{:S(2)}) copy-start(bf16[512,768]{1,0:T(8,128)(2,1)} %param.26) | copy-start | bytes 2359300
  824.8 70.8 %all-gather.7.cloned.1.call-start = ((), (), s32[]{:S(2)}) async-start(), calls=%async_computation.6 | async-start | bytes 3932160 | tf_op jit(solution)/shard_map/all_gather | solution.py:227
  824.8 42.1 %copy-start.37 = (bf16[768,512]{1,0:T(8,128)(2,1)S(1)}, bf16[768,512]{1,0:T(8,128)(2,1)}, u32[]{:S(2)}) copy-start(bf16[768,512]{1,0:T(8,128)(2,1)} %param.37) | copy-start | bytes 2359300
  824.9 212.2 %copy-start.47 = (f32[768]{0:T(1024)}, f32[768]{0:T(1024)S(1)}, u32[]{:S(2)}) copy-start(f32[768]{0:T(1024)S(1)} %convert_element_type.265) | copy-start | bytes 9220
  864.6 172.6 %copy-start.53 = (f32[512]{0:T(512)}, f32[512]{0:T(512)S(1)}, u32[]{:S(2)}) copy-start(f32[512]{0:T(512)S(1)} %fusion.149) | copy-start | bytes 6148
  866.9 80.9 %reduce-scatter.7.cloned.1.call-start = ((), (), s32[]{:S(2)}) async-start(), calls=%async_computation.7 | async-start | bytes 3932160 | tf_op jit(solution)/shard_map/reduce_scatter | solution.py:233
  906.2 41.7 %copy-start.16 = (bf16[512,768]{1,0:T(8,128)(2,1)S(1)}, bf16[512,768]{1,0:T(8,128)(2,1)}, u32[]{:S(2)}) copy-start(bf16[512,768]{1,0:T(8,128)(2,1)} %reduce-scatter.5.cloned.1.call-done) | copy-start | bytes 2359300
  909.7 69.5 %all-gather.9.cloned.1.call-start = ((), (), s32[]{:S(2)}) async-start(), calls=%async_computation.8 | async-start | bytes 3932160 | tf_op jit(solution)/shard_map/all_gather | solution.py:243
  909.8 127.3 %copy-start.51 = (f32[512]{0:T(512)}, f32[512]{0:T(512)S(1)}, u32[]{:S(2)}) copy-start(f32[512]{0:T(512)S(1)} %fusion.147) | copy-start | bytes 6148
  950.6 83.2 %reduce-scatter.9.cloned.1.call-start = ((), (), s32[]{:S(2)}) async-start(), calls=%async_computation.9 | async-start | bytes 3932160 | tf_op jit(solution)/shard_map/reduce_scatter | solution.py:260
  989.2 44.6 %copy-start.24 = (bf16[512,768]{1,0:T(8,128)(2,1)S(1)}, bf16[512,768]{1,0:T(8,128)(2,1)}, u32[]{:S(2)}) copy-start(bf16[512,768]{1,0:T(8,128)(2,1)} %param.27) | copy-start | bytes 2359300
  995.7 71.9 %copy-start.45 = (bf16[192,768]{1,0:T(8,128)(2,1)S(1)}, bf16[192,768]{1,0:T(8,128)(2,1)}, u32[]{:S(2)}) copy-start(bf16[192,768]{1,0:T(8,128)(2,1)} %param.34) | copy-start | bytes 884740
  995.7 71.9 %all-gather.11.cloned.1.call-start = ((), (), s32[]{:S(2)}) async-start(), calls=%async_computation.10 | async-start | bytes 3932160 | tf_op jit(solution)/shard_map/all_gather | solution.py:271
  1037.1 33.5 %copy-start.62 = (f32[512]{0:T(512)}, f32[512]{0:T(512)S(1)}, u32[]{:S(2)}) copy-start(f32[512]{0:T(512)S(1)} %multiply_multiply_fusion.4) | copy-start | bytes 6148
  1038.9 1018.6 %reduce-scatter.11.cloned.1.call-start = ((), (), s32[]{:S(2)}) async-start(), calls=%async_computation.11 | async-start | bytes 3932160 | tf_op jit(solution)/shard_map/reduce_scatter | solution.py:310
  1086.8 7.3 copy-start.2
  1105.8 7.4 copy-start.2
  1125.1 7.3 copy-start.2
  1144.3 7.3 copy-start.2
  1157.9 8.7 copy-start.12
  1157.9 8.7 copy-start.21
  1173.4 7.3 copy-start.4
  1193.6 7.3 copy-start.4
  1214.1 7.4 copy-start.4
  1234.8 7.4 copy-start.4
  1249.0 8.7 copy-start.10
  1249.0 8.7 copy-start.19
  1263.7 7.3 copy-start.6
  1282.2 7.3 copy-start.6
  1301.8 7.4 copy-start.6
  1321.6 7.3 copy-start.6
  1335.2 8.4 copy-start.23
  1335.2 9.9 copy-start.40
  1335.3 9.9 copy-start.42
  1335.3 9.9 copy-start.44
  1349.2 758.0 %all-reduce.17.cloned.1.call-start = ((), (), s32[]{:S(2)}) async-start(), calls=%async_computation.12 | async-start | bytes 14155776 | tf_op jit(solution)/shard_map/psum | solution.py:324
  1349.5 5.0 copy-start.66
  1349.5 5.0 copy-start.69
  1349.5 5.0 copy-start.71
  1354.5 5.1 copy-start.30
  1354.5 5.1 copy-start.32
  1354.5 6.7 copy-start.59
  2050.1 6.7 copy-start.67
  2050.1 7.4 copy-start.14
  2050.1 7.4 copy-start.50
  2050.1 7.4 copy-start.57
  2050.1 9.3 copy-start.64
  2050.2 52.2 %copy-start.61 = (f32[512]{0:T(512)S(1)}, f32[512]{0:T(512)}, u32[]{:S(2)}) copy-start(f32[512]{0:T(512)} %copy-done.60) | copy-start | bytes 6148
  2050.2 53.4 %copy-start.17 = (bf16[512,768]{1,0:T(8,128)(2,1)S(1)}, bf16[512,768]{1,0:T(8,128)(2,1)}, u32[]{:S(2)}) copy-start(bf16[512,768]{1,0:T(8,128)(2,1)} %reduce-scatter.5.cloned.1.call-done) | copy-start | bytes 2359300
  2050.2 53.4 %copy-start.25 = (bf16[512,768]{1,0:T(8,128)(2,1)S(1)}, bf16[512,768]{1,0:T(8,128)(2,1)}, u32[]{:S(2)}) copy-start(bf16[512,768]{1,0:T(8,128)(2,1)} %param.27) | copy-start | bytes 2359300
  2050.2 53.4 %copy-start.27 = (bf16[512,768]{1,0:T(8,128)(2,1)S(1)}, bf16[512,768]{1,0:T(8,128)(2,1)}, u32[]{:S(2)}) copy-start(bf16[512,768]{1,0:T(8,128)(2,1)} %reduce-scatter.7.cloned.1.call-done) | copy-start | bytes 2359300
  2050.2 53.4 %copy-start.48 = (f32[768]{0:T(1024)S(1)}, f32[768]{0:T(1024)}, u32[]{:S(2)}) copy-start(f32[768]{0:T(1024)} %copy-done.47) | copy-start | bytes 9220
  2050.2 53.4 %copy-start.52 = (f32[512]{0:T(512)S(1)}, f32[512]{0:T(512)}, u32[]{:S(2)}) copy-start(f32[512]{0:T(512)} %copy-done.51) | copy-start | bytes 6148
  2050.2 53.4 %copy-start.54 = (f32[512]{0:T(512)S(1)}, f32[512]{0:T(512)}, u32[]{:S(2)}) copy-start(f32[512]{0:T(512)} %copy-done.53) | copy-start | bytes 6148
  2050.2 53.4 %copy-start.63 = (f32[512]{0:T(512)S(1)}, f32[512]{0:T(512)}, u32[]{:S(2)}) copy-start(f32[512]{0:T(512)} %copy-done.62) | copy-start | bytes 6148
  (35 other events, 108.5 us)
Sparse Core Ops, SparseCore 0:
  12.9 28.7 all-gather.4
  824.9 38.1 reduce-scatter.4
  867.0 28.5 all-gather.6
  909.8 37.9 reduce-scatter.6
  950.7 28.5 all-gather.8
  995.8 37.9 reduce-scatter.8
  1039.0 28.5 all-gather.10
  1349.3 37.9 reduce-scatter.10
  1392.9 235.1 all-reduce.16
